TPU v7x, 32 devices: a whole 2x2x4 slice. The times are simulated.
32 devices in a mesh: rep: 4 (over z), shard: 2 (over x), tp: 4 (over y, core).
Axes of the slice: x: 2, y: 2, z: 4, core: 2. Of those that a mesh axis runs over, the one named last changes fastest.
Arguments:
- inner_dense: float32 [4, 2, 768, 3072], P('rep', None, 'shard', 'tp'), may hold values from -6 to 6
- inner_emb: float32 [4, 8192, 768], P('rep', ('shard', 'tp')), may hold values from -6 to 6
- outer_dense: float32 [2, 2, 384, 3072], P(None, 'shard', ('rep', 'tp')), may hold values from -6 to 6
- moment_dense: float32 [2, 2, 384, 3072], P(None, 'shard', ('rep', 'tp')), may hold values from -3 to 3
- outer_emb: float32 [2, 4, 16, 64, 768], P('shard', None, ('rep', 'tp')), may hold values from -6 to 6
- moment_emb: float32 [2, 4, 16, 64, 768], P('shard', None, ('rep', 'tp')), may hold values from -3 to 3
- basis: float32 [64, 768], replicated, may hold values from -0.1875 to 0.1875
Outputs:
- new_outer_dense: float32 [2, 2, 384, 3072], P(None, 'shard', ('rep', 'tp'))
- new_moment_dense: float32 [2, 2, 384, 3072], P(None, 'shard', ('rep', 'tp'))
- new_outer_emb: float32 [2, 4, 16, 64, 768], P('shard', None, ('rep', 'tp'))
- new_moment_emb: float32 [2, 4, 16, 64, 768], P('shard', None, ('rep', 'tp'))
- train_dense: float32 [2, 768, 3072], P(None, 'shard', 'tp')
- train_emb: float32 [8192, 768], P(('shard', 'tp'))
All inputs are finite; a program needn't handle non-finite values.
Results may differ from a plain program's by a relative error of at most 0.00007.
Values sent between devices are 32-bit elements; how exact they have to be, the bound alone decides.
No kernel may reach another device: no remote copies, remote signals or barrier semaphores. Data moves between devices by JAX's collectives and lax.ppermute only.
A program may use at most 64 MiB of HBM per device.

v0:
```python
import jax
import jax.numpy as jnp
from jax import lax
from jax.sharding import PartitionSpec as P

momentum = 0.9
outer_rate = 0.7


def per_device(inner_dense, inner_emb, outer_dense, moment_dense, outer_emb, moment_emb, basis):
    groups = lax.axis_size("rep")
    tp_count = lax.axis_size("tp")
    width = basis.shape[1]
    dense_local = inner_dense[0]
    flat_rows = outer_dense.shape[2]
    piece_rows = outer_emb.shape[3]
    dense_outer = outer_dense[:, 0]
    emb_outer = outer_emb[0, :, 0]
    dense_recv, embed_recv = (
        lax.all_to_all(dense_local, ("rep", "tp"), split_axis=1, concat_axis=2, tiled=True),
        lax.all_to_all(inner_emb, ("rep", "tp"), split_axis=1, concat_axis=2, tiled=True),
    )
    embed_sum = (
        embed_recv.reshape(piece_rows, groups, tp_count, width).sum(axis=1).transpose(1, 0, 2)
    )
    emb_diff = emb_outer - embed_sum / groups
    factors = jnp.einsum(
        "tpd,kd->tpk",
        emb_diff,
        basis,
        precision=lax.Precision.HIGHEST,
        preferred_element_type=jnp.float32,
    )
    dense_sum = dense_recv.reshape(2, flat_rows, groups, -1).sum(axis=2)
    grad_emb = jnp.einsum(
        "tpk,kd->tpd",
        factors,
        basis,
        precision=lax.Precision.HIGHEST,
        preferred_element_type=jnp.float32,
    )
    grad_dense = dense_outer - dense_sum / groups
    moment_new = momentum * moment_dense[:, 0] + grad_dense
    dense_new = dense_outer - outer_rate * (grad_dense + momentum * moment_new)
    emb_moment_new = momentum * moment_emb[0, :, 0] + grad_emb
    emb_new = emb_outer - outer_rate * (grad_emb + momentum * emb_moment_new)
    emb_wide = emb_new.transpose(1, 0, 2).reshape(1, piece_rows, tp_count * width)
    dense_cols, embed_cols = (
        lax.all_to_all(dense_new, "tp", split_axis=2, concat_axis=1, tiled=True),
        lax.all_to_all(emb_wide, "tp", split_axis=2, concat_axis=1, tiled=True),
    )
    dense_train, embed_train = (
        lax.all_gather(dense_cols, "rep", axis=1, tiled=True),
        lax.all_gather(embed_cols, "rep", axis=1, tiled=True),
    )
    return (
        dense_new[:, None],
        moment_new[:, None],
        emb_new[None, :, None],
        emb_moment_new[None, :, None],
        dense_train,
        embed_train[0],
    )


def solution(mesh):
    in_specs = (
        P("rep", None, "shard", "tp"),
        P("rep", ("shard", "tp"), None),
        P(None, "shard", ("rep", "tp"), None),
        P(None, "shard", ("rep", "tp"), None),
        P("shard", None, ("rep", "tp"), None, None),
        P("shard", None, ("rep", "tp"), None, None),
        P(),
    )
    out_specs = (
        P(None, "shard", ("rep", "tp"), None),
        P(None, "shard", ("rep", "tp"), None),
        P("shard", None, ("rep", "tp"), None, None),
        P("shard", None, ("rep", "tp"), None, None),
        P(None, "shard", "tp"),
        P(("shard", "tp"), None),
    )
    return jax.shard_map(
        per_device, mesh=mesh, in_specs=in_specs, out_specs=out_specs, check_vma=False
    )
```

profile of v0, /device:TPU:0, one launch (start us, length us, event | category | flops | bytes accessed | tf_op | source)
XLA Modules:
  0.0 334.2 jit_solution(8532483720370222361)
XLA Ops:
  7.2 3.5 %copy.80 = f32[1,2,384,768]{3,1,2,0:T(2,128)S(1)} copy(f32[1,2,384,768]{3,2,1,0:T(8,128)} %param.7) | data formatting | bytes 4718592 | tf_op args[0]
  10.7 61.2 %all_to_all.66 = f32[2,384,768]{2,0,1:T(2,128)S(1)} all-to-all(f32[2,384,768]{2,0,1:T(2,128)S(1)} %bitcast.130), channel_id=1, replica_groups=mesh['rep'=4,'shard'=2,'tp'=4] {'rep','tp'}, dimensions={1} | all-to-all | bytes 4718592 | tf_op jit(solution)/shard_map/all_to_all | solution.py:20
  71.9 1.4 copy.79
  73.3 2.2 reshape.37
  75.4 3.2 reduce_sum.18
  78.6 0.8 copy-done.1
  79.4 1.0 fusion.6
  80.4 4.2 %copy.63 = f32[2,24,3072]{1,0,2:T(2,128)S(1)} copy(f32[2,24,3072]{2,1,0:T(8,128)} %fusion.6) | data formatting | bytes 1179648 | tf_op jit(solution)/shard_map/sub | solution.py:44
  84.6 6.2 %reshape.41 = f32[4,1,36864]{2,1,0:T(1,128)} reshape(f32[3072,2,24]{2,1,0:T(2,128)S(1)} %bitcast.126) | data formatting | bytes 1179648
  90.9 3.7 %all-to-all-start.2 = ((f32[4,1,36864]{2,1,0:T(1,128)}), f32[4,1,36864]{2,1,0:T(1,128)S(1)}, u32[]{:S(2)}, u32[]{:S(2)}) async-start(f32[4,1,36864]{2,1,0:T(1,128)} %reshape.41), calls=%async_computation.2 | async-start | bytes 1179648 | tf_op jit(solution)/shard_map/all_to_all | solution.py:49
  94.5 6.8 %copy.61 = f32[1,1024,768]{2,0,1:T(1,128)} copy(f32[1,1024,768]{2,1,0:T(8,128)} %param.8) | data formatting | bytes 6291456 | tf_op args[1]
  101.3 2.5 all-to-all-done.2
  103.9 0.8 copy-done.5
  104.7 3.7 %all-to-all-start.1 = ((f32[1,1024,768]{2,0,1:T(1,128)}), f32[1,1024,768]{2,0,1:T(1,128)S(1)}, u32[]{:S(2)}, u32[]{:S(2)}) async-start(f32[1,1024,768]{2,0,1:T(1,128)} %copy.61), calls=%async_computation.1 | async-start | bytes 6291456 | tf_op jit(solution)/shard_map/all_to_all | solution.py:21
  109.0 4.1 %reduce = f32[4,36864]{1,0:T(4,128)} reduce(f32[4,1,36864]{2,1,0:T(1,128)} %copy-done.5, f32[]{:T(128)} %broadcast.54), dimensions={1}, to_apply=%all_to_all.54.reduce_sub_computation | reduce | bytes 1179652 | tf_op jit(solution)/shard_map/all_to_all | solution.py:49
  113.1 7.8 %reshape.42 = f32[3072,2,24]{2,1,0:T(2,128)} reshape(f32[4,36864]{1,0:T(4,128)} %reduce) | data formatting | bytes 1179648
  120.9 5.1 %copy.64 = f32[2,4,24,768]{3,2,1,0:T(8,128)} copy(f32[2,4,24,768]{2,0,3,1:T(2,128)} %bitcast.127) | data formatting | bytes 1179648 | tf_op jit(solution)/shard_map/all_to_all | solution.py:49
  126.2 66.7 %all-to-all-done.1 = f32[1,1024,768]{2,0,1:T(1,128)S(1)} async-done(((f32[1,1024,768]{2,0,1:T(1,128)}), f32[1,1024,768]{2,0,1:T(1,128)S(1)}, u32[]{:S(2)}, u32[]{:S(2)}) %all-to-all-start.1) | async-done | bytes 3145760 | tf_op jit(solution)/shard_map/all_to_all | solution.py:21
  192.9 2.0 copy.76
  194.9 2.3 reduce_sum.19
  197.2 0.8 fusion
  198.0 2.0 fusion.16
  200.5 13.7 %reduce.1 = f32[3072,64]{1,0:T(8,128)S(1)} reduce(f32[3072,1,64]{2,1,0:T(1,128)S(1)} %bitcast.132, f32[]{:T(128)} %broadcast.54), dimensions={1}, to_apply=%bitcast.117.reduce_sub_computation | reduce | bytes 1572868
  214.2 1.0 reshape.43
  215.2 28.2 %all_to_all.67 = f32[4,1,49152]{2,1,0:T(1,128)S(1)} all-to-all(f32[4,1,49152]{2,1,0:T(1,128)S(1)} %reshape.43), channel_id=1, replica_groups=mesh['rep'=4,'shard'=2,'tp'=4] {'tp'}, dimensions={0} | all-to-all | bytes 1572864 | tf_op jit(solution)/shard_map/all_to_all | solution.py:50
  243.4 2.9 reduce.2
  246.3 1.9 reshape.44
  248.7 1.0 copy.68
  250.3 1.2 fusion.9
  251.5 70.9 %all-gather.5.cloned.1.call-done = f32[1,1024,768]{2,1,0:T(8,128)} async-done(((f32[1,256,768]{2,1,0:T(8,128)}), f32[1,1024,768]{2,1,0:T(8,128)}) %all-gather.5.cloned.1.call-update) | async-done | bytes 3145744 | tf_op jit(solution)/shard_map/all_gather | solution.py:54
  322.3 3.4 %copy.83 = f32[2,384,768]{2,1,0:T(8,128)} copy(f32[2,384,768]{2,1,0:T(8,128)} %all-gather.3.cloned.1.call-done) | data formatting | bytes 4718592
  325.7 1.7 copy.84
  (28 shorter events, 2.3 us)
Async XLA Ops:
  7.2 190.0 %copy-start = (f32[64,768]{1,0:T(8,128)S(1)}, f32[64,768]{1,0:T(8,128)}, u32[]{:S(2)}) copy-start(f32[64,768]{1,0:T(8,128)} %param.13) | copy-start | bytes 589828
  75.4 4.0 %copy-start.6 = (f32[2,1,24,3072]{3,2,1,0:T(8,128)S(1)}, f32[2,1,24,3072]{3,2,1,0:T(8,128)}, u32[]{:S(2)}) copy-start(f32[2,1,24,3072]{3,2,1,0:T(8,128)} %param.10) | copy-start | bytes 1769476
  75.4 4.0 %copy-start.8 = (f32[2,1,24,3072]{3,2,1,0:T(8,128)S(1)}, f32[2,1,24,3072]{3,2,1,0:T(8,128)}, u32[]{:S(2)}) copy-start(f32[2,1,24,3072]{3,2,1,0:T(8,128)} %param.9) | copy-start | bytes 1769476
  78.6 0.8 copy-start.1
  90.9 13.0 %all-to-all-start.2 = ((f32[4,1,36864]{2,1,0:T(1,128)}), f32[4,1,36864]{2,1,0:T(1,128)S(1)}, u32[]{:S(2)}, u32[]{:S(2)}) async-start(f32[4,1,36864]{2,1,0:T(1,128)} %reshape.41), calls=%async_computation.2 | async-start | bytes 1179648 | tf_op jit(solution)/shard_map/all_to_all | solution.py:49
  103.9 0.8 copy-start.5
  104.7 88.2 %all-to-all-start.1 = ((f32[1,1024,768]{2,0,1:T(1,128)}), f32[1,1024,768]{2,0,1:T(1,128)S(1)}, u32[]{:S(2)}, u32[]{:S(2)}) async-start(f32[1,1024,768]{2,0,1:T(1,128)} %copy.61), calls=%async_computation.1 | async-start | bytes 6291456 | tf_op jit(solution)/shard_map/all_to_all | solution.py:21
  108.4 143.0 %all-gather.3.cloned.1.call-start = ((), (), s32[]{:S(2)}) async-start(), calls=%async_computation.4 | async-start | bytes 2949120 | tf_op jit(solution)/shard_map/all_gather | solution.py:53
  125.9 196.4 %all-gather.5.cloned.1.call-start = ((), (), s32[]{:S(2)}) async-start(), calls=%async_computation.5 | async-start | bytes 3932160 | tf_op jit(solution)/shard_map/all_gather | solution.py:54
  194.9 2.3 copy-start.4
  194.9 3.1 copy-start.10
  248.2 1.6 copy-start.2
  248.7 1.1 copy-start.7
  248.7 1.6 copy-start.9
  322.3 3.4 %copy-start.3 = (f32[1,1024,768]{2,1,0:T(8,128)S(1)}, f32[1,1024,768]{2,1,0:T(8,128)}, u32[]{:S(2)}) copy-start(f32[1,1024,768]{2,1,0:T(8,128)} %all-gather.5.cloned.1.call-done) | copy-start | bytes 9437188
Sparse Core Ops, SparseCore 0:
  126.1 86.7 all-gather.2
  249.9 72.3 all-gather.4
where the time goes:
time: 335 us; the launch traced here: 334 us
  waiting for transfers between devices  140 us (42%)
  blocking collectives  89.4 us (27%)
  local copies, waits for them, and re-layouts  51.7 us (15%)
  other arithmetic  28.3 us (8%)
  between operations  14.2 us (4%)
  starting transfers between devices  7.7 us (2%)
    all_gather x1, waiting for transfers between devices, per_device(): lax.all_gather(embed_cols, 'rep', axis=1, tiled=True)  70.9 us
    all_to_all x1, waiting for transfers between devices, per_device(): lax.all_to_all(inner_emb, ('rep', 'tp'), split_axis=1, concat_axis=2, til...  66.7 us
    all_to_all x1, blocking collectives, per_device(): lax.all_to_all(dense_local, ('rep', 'tp'), split_axis=1, concat_axis=2, t...  61.2 us
    unnamed x31, local copies, waits for them, and re-layouts  36.4 us
    all_to_all x1, blocking collectives, per_device(): lax.all_to_all(emb_wide, 'tp', split_axis=2, concat_axis=1, tiled=True)  28.2 us
    unnamed x2, other arithmetic  14.9 us
  transfers between devices with their start and end apart: 4, of which 3 were waited for; matrix products, arithmetic and copies ran while one was open for 16% of the time, Pallas kernels for 0%

commit v1 on v0

--- a/solution.py
+++ b/solution.py
@@ -5,6 +5,18 @@
 
 momentum = 0.9
 outer_rate = 0.7
+
+
+def exchange_directly(shard, axis, split, join):
+    ways, here = (lax.axis_size(axis), lax.axis_index(axis))
+    width = shard.shape[split] // ways
+    turned = jnp.roll(shard, -here * width, axis=split)
+    got = [lax.slice_in_dim(turned, 0, width, axis=split)]
+    for far in range(1, ways):
+        sent = lax.slice_in_dim(turned, far * width, (far + 1) * width, axis=split)
+        got.append(lax.ppermute(sent, axis, [(d, (d + far) % ways) for d in range(ways)]))
+    line = jnp.concatenate(got[::-1], axis=join)
+    return jnp.roll(line, (here + 1) * got[0].shape[join], axis=join)
 
 
 def per_device(inner_dense, inner_emb, outer_dense, moment_dense, outer_emb, moment_emb, basis):
@@ -46,7 +58,7 @@
     emb_new = emb_outer - outer_rate * (grad_emb + momentum * emb_moment_new)
     emb_wide = emb_new.transpose(1, 0, 2).reshape(1, piece_rows, tp_count * width)
     dense_cols, embed_cols = (
-        lax.all_to_all(dense_new, "tp", split_axis=2, concat_axis=1, tiled=True),
+        exchange_directly(dense_new, "tp", 2, 1),
         lax.all_to_all(emb_wide, "tp", split_axis=2, concat_axis=1, tiled=True),
     )
     dense_train, embed_train = (

time: 335 us -> 306 us (0.913)
  blocking collectives: 89.4 us -> 27.1 us
  waiting for transfers between devices: 140 us -> 173 us
  starting transfers between devices: 7.7 us -> 22.1 us
  local copies, waits for them, and re-layouts: 51.7 us -> 40.9 us
    all_to_all x1 -> x0, blocking collectives: 61.2 us -> none  [per_device(): lax.all_to_all(dense_local, ('rep', 'tp'), split_axis=1, concat_axis=2, t...]
    all_to_all x1, waiting for transfers between devices: 2.54 us -> 38.9 us  [per_device(): lax.all_to_all(dense_local, ('rep', 'tp'), split_axis=1, concat_axis=2, t...]
    all_to_all x1, waiting for transfers between devices: 66.7 us -> 43.5 us  [per_device(): lax.all_to_all(inner_emb, ('rep', 'tp'), split_axis=1, concat_axis=2, til...]
    ppermute x0 -> x3, waiting for transfers between devices: none -> 15.6 us  [exchange_directly(): lax.ppermute(sent, axis, [(d, (d + far) % ways) for d in range(ways)])]
    all_to_all x1, starting transfers between devices: 3.74 us -> 12.3 us  [per_device(): lax.all_to_all(inner_emb, ('rep', 'tp'), split_axis=1, concat_axis=2, til...]
    unnamed x31 -> x33, local copies, waits for them, and re-layouts: 36.4 us -> 28.2 us
    all_to_all x2 -> x0, local copies, waits for them, and re-layouts: 5.56 us -> none  [per_device(): lax.all_to_all(dense_new, 'tp', split_axis=2, concat_axis=1, tiled=True)]
    sub x1 -> x0, local copies, waits for them, and re-layouts: 4.23 us -> none  [per_device(): dense_new = dense_outer - outer_rate * (grad_dense + momentum * moment_new)]
  transfers between devices with their start and end apart: 4 -> 7, of which waited for: 3 -> 5; matrix products, arithmetic and copies ran while one was open for 16% -> 18% of each run, Pallas kernels for 0% -> 0%
where the time goes in v1:
time: 306 us
  waiting for transfers between devices  173 us (57%)
  local copies, waits for them, and re-layouts  40.9 us (13%)
  blocking collectives  27.1 us (9%)
  other arithmetic  25.9 us (8%)
  starting transfers between devices  22.1 us (7%)
  between operations  14.3 us (5%)
    all_gather x1, waiting for transfers between devices, per_device(): lax.all_gather(embed_cols, 'rep', axis=1, tiled=True)  74.5 us
    all_to_all x1, waiting for transfers between devices, per_device(): lax.all_to_all(inner_emb, ('rep', 'tp'), split_axis=1, concat_axis=2, til...  43.5 us
    all_to_all x1, waiting for transfers between devices, per_device(): lax.all_to_all(dense_local, ('rep', 'tp'), split_axis=1, concat_axis=2, t...  38.9 us
    unnamed x33, local copies, waits for them, and re-layouts  28.2 us
    all_to_all x1, blocking collectives, per_device(): lax.all_to_all(emb_wide, 'tp', split_axis=2, concat_axis=1, tiled=True)  27.1 us
    ppermute x3, waiting for transfers between devices, exchange_directly(): lax.ppermute(sent, axis, [(d, (d + far) % ways) for d in range(ways)])  15.6 us
    unnamed x2, other arithmetic  14.9 us
    all_to_all x1, starting transfers between devices, per_device(): lax.all_to_all(inner_emb, ('rep', 'tp'), split_axis=1, concat_axis=2, til...  12.3 us
  transfers between devices with their start and end apart: 7, of which 5 were waited for; matrix products, arithmetic and copies ran while one was open for 18% of the time, Pallas kernels for 0%

profile of v1, /device:TPU:0, one launch (start us, length us, event | category | flops | bytes accessed | tf_op | source)
XLA Modules:
  0.0 305.6 jit_solution(3761709245409180701)
XLA Ops:
  7.2 4.9 %copy.64 = f32[1,2,384,768]{3,1,2,0:T(2,128)} copy(f32[1,2,384,768]{3,2,1,0:T(8,128)} %param.7) | data formatting | bytes 4718592 | tf_op args[0]
  12.1 7.4 %all-to-all-start = ((f32[2,384,768]{2,0,1:T(2,128)}), f32[2,384,768]{2,0,1:T(2,128)S(1)}, u32[]{:S(2)}, u32[]{:S(2)}) async-start(f32[2,384,768]{2,0,1:T(2,128)} %bitcast.121), calls=%async_computation | async-start | bytes 4718592 | tf_op jit(solution)/shard_map/all_to_all | solution.py:32
  19.5 6.8 %copy.47 = f32[1,1024,768]{2,0,1:T(1,128)} copy(f32[1,1024,768]{2,1,0:T(8,128)} %param.8) | data formatting | bytes 6291456 | tf_op args[1]
  26.3 38.9 %all-to-all-done = f32[2,384,768]{2,0,1:T(2,128)S(1)} async-done(((f32[2,384,768]{2,0,1:T(2,128)}), f32[2,384,768]{2,0,1:T(2,128)S(1)}, u32[]{:S(2)}, u32[]{:S(2)}) %all-to-all-start) | async-done | bytes 2359328 | tf_op jit(solution)/shard_map/all_to_all | solution.py:32
  65.2 1.4 copy-done.1
  66.6 12.3 %all-to-all-start.1 = ((f32[1,1024,768]{2,0,1:T(1,128)}), f32[1,1024,768]{2,0,1:T(1,128)S(1)}, u32[]{:S(2)}, u32[]{:S(2)}) async-start(f32[1,1024,768]{2,0,1:T(1,128)} %copy.47), calls=%async_computation.1 | async-start | bytes 6291456 | tf_op jit(solution)/shard_map/all_to_all | solution.py:33
  78.9 4.5 %copy.63 = f32[2,16,24,768]{3,1,2,0:T(8,128)} copy(f32[2,16,24,768]{3,0,2,1:T(2,128)} %bitcast.120) | data formatting | bytes 4718592 | tf_op jit(solution)/shard_map/all_to_all | solution.py:32
  83.4 3.7 %reshape.37 = f32[2,24,4,3072]{3,2,1,0:T(4,128)} reshape(f32[2,24,16,768]{3,2,1,0:T(8,128)} %bitcast.122) | data formatting | bytes 4718592 | tf_op jit(solution)/shard_map/reshape | solution.py:46
  87.1 3.9 %reduce_sum.18 = f32[2,24,3072]{2,1,0:T(8,128)} reduce(f32[2,24,4,3072]{3,2,1,0:T(4,128)} %reshape.37, f32[]{:T(128)} %constant.45.clone.1), dimensions={2}, to_apply=%region_0.0 | reduce | flops 442368 | bytes 2949124 | tf_op jit(solution)/shard_map/reduce_sum | solution.py:46
  91.0 1.6 fusion.7
  94.6 1.7 collective-permute-start
  96.8 5.3 %collective-permute-done = f32[2,24,768]{2,1,0:T(8,128)S(1)} collective-permute-done((f32[2,24,768]{2,1,0:T(8,128)}, f32[2,24,768]{2,1,0:T(8,128)S(1)}, u32[]{:S(2)}, u32[]{:S(2)}) %collective-permute-start) | collective-permute-done | bytes 147488 | tf_op jit(solution)/shard_map/ppermute | solution.py:17
  102.1 10.3 %collective-permute-done.1 = f32[2,24,768]{2,1,0:T(8,128)} collective-permute-done((f32[2,24,768]{2,1,0:T(8,128)}, f32[2,24,768]{2,1,0:T(8,128)}, u32[]{:S(2)}, u32[]{:S(2)}) %collective-permute-start.1) | collective-permute-done | bytes 147488 | tf_op jit(solution)/shard_map/ppermute | solution.py:17
  112.4 0.9 constant_dynamic-update-slice_fusion.4
  113.4 0.9 slice_dynamic-update-slice_fusion
  114.3 0.9 constant_dynamic-update-slice_fusion.1
  115.2 0.9 slice_dynamic-update-slice_fusion.1
  116.2 0.9 constant_dynamic-slice_fusion
  117.3 43.5 %all-to-all-done.1 = f32[1,1024,768]{2,0,1:T(1,128)S(1)} async-done(((f32[1,1024,768]{2,0,1:T(1,128)}), f32[1,1024,768]{2,0,1:T(1,128)S(1)}, u32[]{:S(2)}, u32[]{:S(2)}) %all-to-all-start.1) | async-done | bytes 3145760 | tf_op jit(solution)/shard_map/all_to_all | solution.py:33
  160.8 2.0 copy.60
  162.8 2.2 reduce_sum.19
  166.2 2.0 fusion.17
  169.2 13.7 %reduce = f32[3072,64]{1,0:T(8,128)S(1)} reduce(f32[3072,1,64]{2,1,0:T(1,128)S(1)} %bitcast.124, f32[]{:T(128)} %broadcast.54), dimensions={1}, to_apply=%bitcast.111.reduce_sub_computation | reduce | bytes 1572868
  182.9 1.0 reshape.41
  183.9 27.1 %all_to_all.48 = f32[4,1,49152]{2,1,0:T(1,128)S(1)} all-to-all(f32[4,1,49152]{2,1,0:T(1,128)S(1)} %reshape.41), channel_id=1, replica_groups=mesh['rep'=4,'shard'=2,'tp'=4] {'tp'}, dimensions={0} | all-to-all | bytes 1572864 | tf_op jit(solution)/shard_map/all_to_all | solution.py:62
  211.0 2.9 reduce.1
  214.0 1.9 reshape.42
  216.4 1.0 copy.52
  218.1 1.2 fusion.10
  219.3 74.5 %all-gather.5.cloned.1.call-done = f32[1,1024,768]{2,1,0:T(8,128)} async-done(((f32[1,256,768]{2,1,0:T(8,128)}), f32[1,1024,768]{2,1,0:T(8,128)}) %all-gather.5.cloned.1.call-update) | async-done | bytes 3145744 | tf_op jit(solution)/shard_map/all_gather | solution.py:66
  293.7 3.4 %copy.74 = f32[2,384,768]{2,1,0:T(8,128)} copy(f32[2,384,768]{2,1,0:T(8,128)} %all-gather.3.cloned.1.call-done) | data formatting | bytes 4718592
  297.1 1.7 copy.75
  (35 shorter events, 6.1 us)
Async XLA Ops:
  7.2 157.9 %copy-start = (f32[64,768]{1,0:T(8,128)S(1)}, f32[64,768]{1,0:T(8,128)}, u32[]{:S(2)}) copy-start(f32[64,768]{1,0:T(8,128)} %param.13) | copy-start | bytes 589828
  12.1 53.1 %all-to-all-start = ((f32[2,384,768]{2,0,1:T(2,128)}), f32[2,384,768]{2,0,1:T(2,128)S(1)}, u32[]{:S(2)}, u32[]{:S(2)}) async-start(f32[2,384,768]{2,0,1:T(2,128)} %bitcast.121), calls=%async_computation | async-start | bytes 4718592 | tf_op jit(solution)/shard_map/all_to_all | solution.py:32
  65.2 1.4 copy-start.1
  66.6 94.2 %all-to-all-start.1 = ((f32[1,1024,768]{2,0,1:T(1,128)}), f32[1,1024,768]{2,0,1:T(1,128)S(1)}, u32[]{:S(2)}, u32[]{:S(2)}) async-start(f32[1,1024,768]{2,0,1:T(1,128)} %copy.47), calls=%async_computation.1 | async-start | bytes 6291456 | tf_op jit(solution)/shard_map/all_to_all | solution.py:33
  78.9 140.4 %all-gather.3.cloned.1.call-start = ((), (), s32[]{:S(2)}) async-start(), calls=%async_computation.3 | async-start | bytes 2949120 | tf_op jit(solution)/shard_map/all_gather | solution.py:65
  93.0 0.8 copy-start.5
  94.6 7.5 %collective-permute-start = (f32[2,24,768]{2,1,0:T(8,128)}, f32[2,24,768]{2,1,0:T(8,128)S(1)}, u32[]{:S(2)}, u32[]{:S(2)}) collective-permute-start(f32[2,24,768]{2,1,0:T(8,128)} %get-tuple-element.37), channel_id=1, source_target_pairs={{0,3},{1,0},{2,1},{3,2},{4,7},{5,4},{6,5},{7,6},{8,11},{9,8},{10,9... | collective-permute-start | bytes 442376 | tf_op jit(solution)/shard_map/ppermute | solution.py:17
  96.2 16.2 %collective-permute-start.1 = (f32[2,24,768]{2,1,0:T(8,128)}, f32[2,24,768]{2,1,0:T(8,128)}, u32[]{:S(2)}, u32[]{:S(2)}) collective-permute-start(f32[2,24,768]{2,1,0:T(8,128)} %get-tuple-element.36), channel_id=1, source_target_pairs={{0,2},{1,3},{2,0},{3,1},{4,6},{5,7},{6,4},{7,5},{8,10},{9,11},{10,... | collective-permute-start | bytes 442376 | tf_op jit(solution)/shard_map/ppermute | solution.py:17
  96.6 16.7 %collective-permute-start.2 = (f32[2,24,768]{2,1,0:T(8,128)}, f32[2,24,768]{2,1,0:T(8,128)S(1)}, u32[]{:S(2)}, u32[]{:S(2)}) collective-permute-start(f32[2,24,768]{2,1,0:T(8,128)} %get-tuple-element.35), channel_id=1, source_target_pairs={{0,1},{1,2},{2,3},{3,0},{4,5},{5,6},{6,7},{7,4},{8,9},{9,10},{10,1... | collective-permute-start | bytes 442376 | tf_op jit(solution)/shard_map/ppermute | solution.py:17
  117.1 176.7 %all-gather.5.cloned.1.call-start = ((), (), s32[]{:S(2)}) async-start(), calls=%async_computation.4 | async-start | bytes 3932160 | tf_op jit(solution)/shard_map/all_gather | solution.py:66
  162.8 2.2 copy-start.4
  165.0 1.1 copy-start.8
  216.4 1.1 copy-start.2
  216.4 1.5 copy-start.6
  216.4 1.7 copy-start.7
  293.7 3.4 %copy-start.3 = (f32[1,1024,768]{2,1,0:T(8,128)S(1)}, f32[1,1024,768]{2,1,0:T(8,128)}, u32[]{:S(2)}) copy-start(f32[1,1024,768]{2,1,0:T(8,128)} %all-gather.5.cloned.1.call-done) | copy-start | bytes 9437188
Sparse Core Ops, SparseCore 0:
  117.2 66.8 all-gather.2
  217.6 76.1 all-gather.4
